TPU v7x, 256 devices: a whole 4x4x8 slice. The times are simulated.
256 devices in a mesh: section: 2 (over z_hi), dp: 16 (over z_lo, y), tensor: 8 (over x, core).
Axes of the slice: x: 4, y: 4, z: 8 (z_hi: 2, z_lo: 4; z = z_hi * 4 + z_lo), core: 2. Of those that a mesh axis runs over, the one named last changes fastest.
Arguments:
- section_input: bfloat16 [2, 1024, 8192], P('section', 'tensor', 'dp'), may hold values from -40 to 40
- norm_gain_attn: bfloat16 [2, 8192], P('section', 'dp'), may hold values from 0.099609375 to 1.8984375
- w_query: bfloat16 [2, 8192, 4096], P('section', 'dp', 'tensor'), may hold values from -0.0625 to 0.0625
- key_value_weight: bfloat16 [2, 2, 8192, 512], P('section', None, 'dp'), may hold values from -0.0625 to 0.0625
- w_output: bfloat16 [2, 4096, 8192], P('section', 'tensor', 'dp'), may hold values from -0.09375 to 0.09375
- norm_gain_ffn: bfloat16 [2, 8192], P('section', 'dp'), may hold values from 0.099609375 to 1.8984375
- w_gate_up: bfloat16 [2, 2, 8192, 14336], P('section', None, 'dp', 'tensor'), may hold values from -0.0625 to 0.0625
- w_down: bfloat16 [2, 14336, 8192], P('section', 'tensor', 'dp'), may hold values from -0.046875 to 0.046875
Outputs:
- section_output: bfloat16 [2, 1024, 8192], P('section', 'tensor', 'dp')
All inputs are finite; a program needn't handle non-finite values.
Results may differ from a plain program's by a relative error of at most 0.019.
Values may be sent and summed in bfloat16 or wider, within the bound.
A program may use at most 64 MiB of HBM per device.

v0:
```python
import math
import jax
import jax.numpy as jnp
from jax import lax
from jax.sharding import PartitionSpec as P

HEAD_SIZE = 128
QUERY_HEADS = 32
KEY_VALUE_HEADS = 4
EPS = 1e-05
THETA = 500000.0


def from_behind(x, axis, by):
    count = lax.axis_size(axis)
    return lax.ppermute(x, axis, [(i, (i + by) % count) for i in range(count)])


def apply_rotary(value_states, token_positions):
    width = value_states.shape[-1]
    half = width // 2
    freqs = jnp.exp(-(2.0 * jnp.arange(half, dtype=jnp.float32) / width) * math.log(THETA))
    angles = token_positions.astype(jnp.float32)[:, None] * freqs[None, :]
    cosine = jnp.cos(angles)[:, None, :]
    sine = jnp.sin(angles)[:, None, :]
    first = value_states[..., :half]
    second = value_states[..., half:]
    return jnp.concatenate(
        [first * cosine - second * sine, second * cosine + first * sine], axis=-1
    )


def local(
    section_input,
    norm_gain_attn,
    w_query,
    key_value_weight,
    w_output,
    norm_gain_ffn,
    w_gate_up,
    w_down,
):
    tile = section_input[0]
    rows_dev = tile.shape[0]
    cols_dev = tile.shape[1]
    tensor_count = lax.axis_size("tensor")
    data_count = lax.axis_size("dp")
    seq_total = rows_dev * tensor_count
    query_rows = seq_total // data_count
    width_total = cols_dev * data_count
    head_dim = HEAD_SIZE
    heads_dev = w_query.shape[2] // head_dim
    group_heads = QUERY_HEADS // KEY_VALUE_HEADS
    kv_dev = max(1, heads_dev // group_heads)
    per_kv = heads_dev // kv_dev
    tensor_pos = lax.axis_index("tensor")
    data_pos = lax.axis_index("dp")
    kv_first = tensor_pos * heads_dev // group_heads
    key_cols = lax.dynamic_slice_in_dim(
        key_value_weight[0], kv_first * head_dim, kv_dev * head_dim, 2
    )
    w_columns = jnp.concatenate([w_query[0], key_cols[0], key_cols[1]], axis=1)
    gain_attn = norm_gain_attn[0].astype(jnp.float32)[None, :]
    gain_ffn = norm_gain_ffn[0].astype(jnp.float32)[None, :]
    query_cols = heads_dev * head_dim
    kv_cols = kv_dev * head_dim
    query_pos = data_pos * query_rows + jnp.arange(query_rows, dtype=jnp.int32)
    all_pos = jnp.arange(seq_total, dtype=jnp.int32)
    arrived = from_behind(tile, "section", 1)
    wide = arrived.astype(jnp.float32)
    squares = lax.psum(jnp.sum(wide * wide, axis=1), "dp")
    normed_input = (wide * lax.rsqrt(squares / width_total + EPS)[:, None] * gain_attn).astype(
        jnp.bfloat16
    )
    partial_qkv = jnp.dot(
        lax.all_gather(normed_input, "tensor", axis=0, tiled=True),
        w_columns,
        preferred_element_type=jnp.float32,
    )
    query_sum = lax.psum_scatter(
        partial_qkv[:, :query_cols].astype(jnp.bfloat16), "dp", scatter_dimension=0, tiled=True
    ).astype(jnp.float32)
    key_sum = lax.psum(partial_qkv[:, query_cols:].astype(jnp.bfloat16), "dp").astype(jnp.float32)
    keys = apply_rotary(key_sum[:, :kv_cols].reshape(seq_total, kv_dev, head_dim), all_pos).astype(
        jnp.bfloat16
    )
    value_states = key_sum[:, kv_cols:].reshape(seq_total, kv_dev, head_dim).astype(jnp.bfloat16)
    query_states = apply_rotary(
        query_sum.reshape(query_rows, heads_dev, head_dim), query_pos
    ).astype(jnp.bfloat16)
    grouped = query_states.reshape(query_rows, kv_dev, per_kv, head_dim)
    scores = jnp.einsum(
        "qkgd,skd->kgqs", grouped, keys, preferred_element_type=jnp.float32
    ) * head_dim ** (-0.5)
    visible = all_pos[None, :] <= query_pos[:, None]
    weights_exp = jnp.where(visible, jnp.exp(scores), 0.0)
    probs = (weights_exp / jnp.sum(weights_exp, axis=-1, keepdims=True)).astype(jnp.bfloat16)
    mixed = (
        jnp.einsum("kgqs,skd->qkgd", probs, value_states, preferred_element_type=jnp.float32)
        .astype(jnp.bfloat16)
        .reshape(query_rows, query_cols)
    )
    attn_partial = jnp.dot(
        lax.all_gather(mixed, "dp", axis=0, tiled=True),
        w_output[0],
        preferred_element_type=jnp.float32,
    )
    attn = lax.psum_scatter(
        attn_partial.astype(jnp.bfloat16), "tensor", scatter_dimension=0, tiled=True
    ).astype(jnp.float32)
    resid = (arrived.astype(jnp.float32) + attn).astype(jnp.bfloat16)
    resid_wide = resid.astype(jnp.float32)
    squares_ffn = lax.psum(jnp.sum(resid_wide * resid_wide, axis=1), "dp")
    normed_ffn = (
        resid_wide * lax.rsqrt(squares_ffn / width_total + EPS)[:, None] * gain_ffn
    ).astype(jnp.bfloat16)
    rows_ffn = lax.all_gather(normed_ffn, "tensor", axis=0, tiled=True)
    ff_dev = w_gate_up.shape[3]
    summed = lax.psum_scatter(
        jnp.einsum("rd,gdf->rgf", rows_ffn, w_gate_up[0], preferred_element_type=jnp.float32)
        .reshape(query_rows * lax.axis_size("dp"), 2 * ff_dev)
        .astype(jnp.bfloat16),
        "dp",
        scatter_dimension=0,
        tiled=True,
    ).astype(jnp.float32)
    hidden = (jax.nn.silu(summed[:, :ff_dev]) * summed[:, ff_dev:]).astype(jnp.bfloat16)
    ffn_partial = jnp.dot(
        lax.all_gather(hidden, "dp", axis=0, tiled=True),
        w_down[0],
        preferred_element_type=jnp.float32,
    )
    ffn = lax.psum_scatter(
        ffn_partial.astype(jnp.bfloat16), "tensor", scatter_dimension=0, tiled=True
    ).astype(jnp.float32)
    result = (resid_wide + ffn).astype(jnp.bfloat16)
    return result[None]


def solution(mesh):
    placed = (
        P("section", "tensor", "dp"),
        P("section", "dp"),
        P("section", "dp", "tensor"),
        P("section", None, "dp", None),
        P("section", "tensor", "dp"),
        P("section", "dp"),
        P("section", None, "dp", "tensor"),
        P("section", "tensor", "dp"),
    )
    return jax.shard_map(
        local, mesh=mesh, in_specs=placed, out_specs=P("section", "tensor", "dp"), check_vma=False
    )
```

profile of v0, /device:TPU:8, one launch (start us, length us, event | category | flops | bytes accessed | tf_op | source)
XLA Modules:
  0.0 766.1 jit_solution(4502816704359785971)
XLA Ops:
  6.5 0.0 copy-start
  6.5 0.0 all-gather.5.cloned.1.call-start
  6.5 7.2 collective-permute-start
  13.7 0.7 mul.231
  14.4 3.1 collective-permute-done
  17.5 0.1 fusion.25
  17.6 38.6 %psum.21 = f32[128]{0:T(128)S(1)} all-reduce(f32[128]{0:T(128)S(1)} %fusion.25), channel_id=1, replica_groups=mesh['section'=2,'dp'=16,'tensor'=8] {'dp'}, use_global_device_ids=true, to_apply=%region_1.2 | all-reduce | flops 128 | bytes 1024 | tf_op jit(solution)/shard_map/psum | solution.py:71
  56.2 0.8 fusion.27
  57.0 0.0 all-gather.5.cloned.1.call-update
  57.0 0.0 all-reduce.2.cloned.1.call-start
  57.1 1.7 dynamic-slice_bitcast_fusion.1
  58.8 27.4 %all-gather.5.cloned.1.call-done = bf16[1024,512]{1,0:T(8,128)(2,1)} async-done(((bf16[128,512]{1,0:T(8,128)(2,1)}), bf16[1024,512]{1,0:T(8,128)(2,1)}) %all-gather.5.cloned.1.call-update) | async-done | bytes 1048592 | tf_op jit(solution)/shard_map/all_gather | solution.py:76
  86.2 2.4 convolution_convert_fusion.1
  88.7 0.8 slice.54
  89.5 0.0 all-reduce.2.cloned.1.call-update
  89.5 0.0 reduce-scatter.5.cloned.1.call-start
  89.6 1.0 slice.59
  90.6 0.0 reduce-scatter.5.cloned.1.call-update
  90.7 0.0 all-gather.7.cloned.1.call-start
  90.8 0.1 iota_compare_fusion
  90.9 0.2 multiply_cosine_fusion.1
  91.1 160.4 %all-reduce.2.cloned.1.call-done = bf16[1024,256]{1,0:T(8,128)(2,1)} async-done(((bf16[1024,256]{1,0:T(8,128)(2,1)}), bf16[1024,256]{1,0:T(8,128)(2,1)}) %all-reduce.2.cloned.1.call-update) | async-done | bytes 524304 | tf_op jit(solution)/shard_map/psum | solution.py:83
  251.5 1.1 fusion.33
  252.6 2.4 fusion.37
  255.0 79.3 %reduce-scatter.5.cloned.1.call-done = bf16[64,512]{1,0:T(8,128)(2,1)} async-done(((bf16[1024,512]{1,0:T(8,128)(2,1)}), bf16[64,512]{1,0:T(8,128)(2,1)}) %reduce-scatter.5.cloned.1.call-update) | async-done | bytes 65552 | tf_op jit(solution)/shard_map/reduce_scatter | solution.py:80
  334.3 0.9 reshape.220
  335.2 0.1 fusion.45
  335.4 0.6 fusion.46
  336.0 0.0 copy-done.2
  336.0 0.4 fusion.8
  336.3 0.0 copy-start.3
  336.4 0.1 copy.13
  336.4 0.6 copy.23
  337.1 0.0 all-gather.7.cloned.1.call-update
  337.1 0.0 reduce-scatter.7.cloned.1.call-start
  337.1 81.5 %all-gather.7.cloned.1.call-done = bf16[1024,512]{1,0:T(8,128)(2,1)} async-done(((bf16[64,512]{1,0:T(8,128)(2,1)}), bf16[1024,512]{1,0:T(8,128)(2,1)}) %all-gather.7.cloned.1.call-update) | async-done | bytes 1048592 | tf_op jit(solution)/shard_map/all_gather | solution.py:104
  418.6 3.0 convolution_convert_fusion.2
  421.7 0.0 reduce-scatter.7.cloned.1.call-update
  421.7 0.0 all-gather.9.cloned.1.call-start
  421.7 0.0 copy-done.3
  421.8 33.3 %reduce-scatter.7.cloned.1.call-done = bf16[128,512]{1,0:T(8,128)(2,1)} async-done(((bf16[1024,512]{1,0:T(8,128)(2,1)}), bf16[128,512]{1,0:T(8,128)(2,1)}) %reduce-scatter.7.cloned.1.call-update) | async-done | bytes 131088 | tf_op jit(solution)/shard_map/reduce_scatter | solution.py:108
  455.1 1.0 fusion.29
  456.1 39.0 %psum.23 = f32[128]{0:T(128)S(1)} all-reduce(f32[128]{0:T(128)S(1)} %fusion.29), channel_id=1, replica_groups=mesh['section'=2,'dp'=16,'tensor'=8] {'dp'}, use_global_device_ids=true, to_apply=%region_7.8 | all-reduce | flops 128 | bytes 1024 | tf_op jit(solution)/shard_map/psum | solution.py:113
  495.1 1.7 fusion.31
  496.7 0.0 all-gather.9.cloned.1.call-update
  496.7 0.0 reduce-scatter.9.cloned.1.call-start
  496.8 6.0 copy.14
  502.8 18.1 %all-gather.9.cloned.1.call-done = bf16[1024,512]{1,0:T(8,128)(2,1)} async-done(((bf16[128,512]{1,0:T(8,128)(2,1)}), bf16[1024,512]{1,0:T(8,128)(2,1)}) %all-gather.9.cloned.1.call-update) | async-done | bytes 1048592 | tf_op jit(solution)/shard_map/all_gather | solution.py:117
  520.9 9.3 %convolution_convert_fusion = bf16[1024,3584]{1,0:T(8,128)(2,1)} fusion(bf16[1024,512]{1,0:T(8,128)(2,1)} %all-gather.9.cloned.1.call-done, bf16[3584,512]{1,0:T(8,128)(2,1)} %bitcast.64), kind=kOutput, calls=%fused_computation | convolution fusion | flops 3761766400 | bytes 12058624 | tf_op jit(solution)/shard_map/rd,gdf->rgf/dot_general | solution.py:120
  530.2 0.0 reduce-scatter.9.cloned.1.call-update
  530.3 0.0 all-gather.11.cloned.1.call-start
  530.3 101.4 %reduce-scatter.9.cloned.1.call-done = bf16[64,3584]{1,0:T(8,128)(2,1)} async-done(((bf16[1024,3584]{1,0:T(8,128)(2,1)}), bf16[64,3584]{1,0:T(8,128)(2,1)}) %reduce-scatter.9.cloned.1.call-update) | async-done | bytes 458768 | tf_op jit(solution)/shard_map/reduce_scatter | solution.py:119
  631.7 1.1 convert_element_type.103
  632.8 0.8 fusion.24
  633.6 0.0 all-gather.11.cloned.1.call-update
  633.6 0.0 copy-start.1
  633.6 0.0 reduce-scatter.11.cloned.1.call-start
  633.7 85.8 %all-gather.11.cloned.1.call-done = bf16[1024,1792]{1,0:T(8,128)(2,1)} async-done(((bf16[64,1792]{1,0:T(8,128)(2,1)}), bf16[1024,1792]{1,0:T(8,128)(2,1)}) %all-gather.11.cloned.1.call-update) | async-done | bytes 3670032 | tf_op jit(solution)/shard_map/all_gather | solution.py:129
  719.4 0.0 copy-done
  719.4 5.1 fusion.2
  724.5 0.0 reduce-scatter.11.cloned.1.call-update
  724.5 33.5 %reduce-scatter.11.cloned.1.call-done = bf16[128,512]{1,0:T(8,128)(2,1)} async-done(((bf16[1024,512]{1,0:T(8,128)(2,1)}), bf16[128,512]{1,0:T(8,128)(2,1)}) %reduce-scatter.11.cloned.1.call-update) | async-done | bytes 131088 | tf_op jit(solution)/shard_map/reduce_scatter | solution.py:133
  758.0 0.0 copy-done.1
  758.0 1.6 fusion.38
  (9 shorter events, 0.1 us)
Async XLA Ops:
  6.5 712.9 %copy-start = (bf16[1,1792,512]{2,1,0:T(8,128)(2,1)S(1)}, bf16[1,1792,512]{2,1,0:T(8,128)(2,1)}, u32[]{:S(2)}) copy-start(bf16[1,1792,512]{2,1,0:T(8,128)(2,1)} %param.15) | copy-start | bytes 5505028
  6.5 79.7 %all-gather.5.cloned.1.call-start = ((), (), s32[]{:S(2)}) async-start(), calls=%async_computation.4 | async-start | bytes 1179648 | tf_op jit(solution)/shard_map/all_gather | solution.py:76
  6.5 11.0 %collective-permute-start = (bf16[128,512]{1,0:T(8,128)(2,1)}, bf16[128,512]{1,0:T(8,128)(2,1)S(1)}, u32[]{:S(2)}, u32[]{:S(2)}) collective-permute-start(bf16[128,512]{1,0:T(8,128)(2,1)} %bitcast.70), channel_id=1, source_target_pairs={{0,128},{128,0},{1,129},{129,1},{2,130},{130,2},{3,131},{131,3},{4... | collective-permute-start | bytes 393224 | tf_op jit(solution)/shard_map/ppermute | solution.py:16
  57.0 194.5 %all-reduce.2.cloned.1.call-start = ((), (), s32[]{:S(2)}) async-start(), calls=%async_computation.5 | async-start | bytes 1048576 | tf_op jit(solution)/shard_map/psum | solution.py:83
  89.5 244.8 %reduce-scatter.5.cloned.1.call-start = ((), (), s32[]{:S(2)}) async-start(), calls=%async_computation.6 | async-start | bytes 1114112 | tf_op jit(solution)/shard_map/reduce_scatter | solution.py:80
  90.7 328.0 %all-gather.7.cloned.1.call-start = ((), (), s32[]{:S(2)}) async-start(), calls=%async_computation.7 | async-start | bytes 1114112 | tf_op jit(solution)/shard_map/all_gather | solution.py:104
  251.5 84.5 %copy-start.2 = (bf16[1024,256]{1,0:T(8,128)(2,1)S(1)}, bf16[1024,256]{1,0:T(8,128)(2,1)}, u32[]{:S(2)}) copy-start(bf16[1024,256]{1,0:T(8,128)(2,1)} %all-reduce.2.cloned.1.call-done) | copy-start | bytes 1572868
  336.3 85.4 %copy-start.3 = (bf16[1,512]{1,0:T(2,128)(2,1)S(1)}, bf16[1,512]{1,0:T(2,128)(2,1)}, u32[]{:S(2)}) copy-start(bf16[1,512]{1,0:T(2,128)(2,1)} %param.13) | copy-start | bytes 3076
  337.1 118.0 %reduce-scatter.7.cloned.1.call-start = ((), (), s32[]{:S(2)}) async-start(), calls=%async_computation.8 | async-start | bytes 1179648 | tf_op jit(solution)/shard_map/reduce_scatter | solution.py:108
  421.7 99.2 %all-gather.9.cloned.1.call-start = ((), (), s32[]{:S(2)}) async-start(), calls=%async_computation.9 | async-start | bytes 1179648 | tf_op jit(solution)/shard_map/all_gather | solution.py:117
  496.7 134.9 %reduce-scatter.9.cloned.1.call-start = ((), (), s32[]{:S(2)}) async-start(), calls=%async_computation.10 | async-start | bytes 7798784 | tf_op jit(solution)/shard_map/reduce_scatter | solution.py:119
  530.3 189.1 %all-gather.11.cloned.1.call-start = ((), (), s32[]{:S(2)}) async-start(), calls=%async_computation.11 | async-start | bytes 3899392 | tf_op jit(solution)/shard_map/all_gather | solution.py:129
  633.6 124.4 %copy-start.1 = (bf16[128,512]{1,0:T(8,128)(2,1)S(1)}, bf16[128,512]{1,0:T(8,128)(2,1)}, u32[]{:S(2)}) copy-start(bf16[128,512]{1,0:T(8,128)(2,1)} %reduce-scatter.7.cloned.1.call-done) | copy-start | bytes 393220
  633.6 124.4 %reduce-scatter.11.cloned.1.call-start = ((), (), s32[]{:S(2)}) async-start(), calls=%async_computation.12 | async-start | bytes 1179648 | tf_op jit(solution)/shard_map/reduce_scatter | solution.py:133
Sparse Core Ops, SparseCore 0:
  57.2 29.0 all-gather.4
  89.7 161.8 all-reduce.1
  254.0 80.2 reduce-scatter.4
  337.2 81.3 all-gather.6
  421.8 33.1 reduce-scatter.6
  496.9 24.0 all-gather.8
  530.4 101.2 reduce-scatter.8
  633.7 85.6 all-gather.10
  724.7 33.2 reduce-scatter.10
where the time goes:
time: 767 us; the launch traced here: 766 us
  waiting for transfers between devices  624 us (81%)
  blocking collectives  77.6 us (10%)
  matrix products  20.8 us (3%)
  between operations  13.4 us (2%)
  other arithmetic  11.6 us (2%)
  local copies, waits for them, and re-layouts  11.3 us (1%)
    psum x1, waiting for transfers between devices, local(): lax.psum(partial_qkv[:, query_cols:].astype(jnp.bfloat16), 'dp')  160 us
    reduce_scatter x1, waiting for transfers between devices, local(): lax.psum_scatter(jnp.einsum('rd,gdf->rgf', rows_ffn, w_gate_up[0], prefer...  101 us
    all_gather x1, waiting for transfers between devices, local(): lax.all_gather(hidden, 'dp', axis=0, tiled=True)  85.8 us
    all_gather x1, waiting for transfers between devices, local(): lax.all_gather(mixed, 'dp', axis=0, tiled=True)  81.5 us
    reduce_scatter x1, waiting for transfers between devices, local(): lax.psum_scatter(partial_qkv[:, :query_cols].astype(jnp.bfloat16), 'dp',...  79.3 us
    psum x1, blocking collectives, local(): squares_ffn = lax.psum(jnp.sum(resid_wide * resid_wide, axis=1), 'dp')  39 us
    psum x1, blocking collectives, local(): squares = lax.psum(jnp.sum(wide * wide, axis=1), 'dp')  38.6 us
    reduce_scatter x1, waiting for transfers between devices, local(): lax.psum_scatter(ffn_partial.astype(jnp.bfloat16), 'tensor', scatter_dime...  33.5 us
  transfers between devices with their start and end apart: 10, of which 10 were waited for; matrix products, arithmetic and copies ran while one was open for 2% of the time, Pallas kernels for 0%

commit v1 on v0

--- a/solution.py
+++ b/solution.py
@@ -101,7 +101,9 @@
         .reshape(query_rows, query_cols)
     )
     attn_partial = jnp.dot(
-        lax.all_gather(mixed, "dp", axis=0, tiled=True),
+        jnp.concatenate(
+            lax.all_to_all(jnp.stack([mixed] * lax.axis_size("dp")), "dp", 0, 0), axis=0
+        ),
         w_output[0],
         preferred_element_type=jnp.float32,
     )

time: 767 us -> 708 us (0.923)
  waiting for transfers between devices: 624 us -> 544 us
  blocking collectives: 77.6 us -> 101 us
    all_gather x1 -> x0, waiting for transfers between devices: 81.5 us -> none  [local(): lax.all_gather(mixed, 'dp', axis=0, tiled=True)]
    all_to_all x0 -> x1, blocking collectives: none -> 23.4 us  [local(): lax.all_to_all(jnp.stack([mixed] * lax.axis_size('dp')), 'dp', 0, 0)]
  transfers between devices with their start and end apart: 10 -> 9, of which waited for: 10 -> 9; matrix products, arithmetic and copies ran while one was open for 2% -> 2% of each run, Pallas kernels for 0% -> 0%
where the time goes in v1:
time: 708 us
  waiting for transfers between devices  544 us (77%)
  blocking collectives  101 us (14%)
  matrix products  19.4 us (3%)
  between operations  13.7 us (2%)
  other arithmetic  11.6 us (2%)
  local copies, waits for them, and re-layouts  10.8 us (2%)
  starting transfers between devices  7.48 us (1%)
    psum x1, waiting for transfers between devices, local(): lax.psum(partial_qkv[:, query_cols:].astype(jnp.bfloat16), 'dp')  160 us
    reduce_scatter x1, waiting for transfers between devices, local(): lax.psum_scatter(jnp.einsum('rd,gdf->rgf', rows_ffn, w_gate_up[0], prefer...  101 us
    all_gather x1, waiting for transfers between devices, local(): lax.all_gather(hidden, 'dp', axis=0, tiled=True)  86.1 us
    reduce_scatter x1, waiting for transfers between devices, local(): lax.psum_scatter(partial_qkv[:, :query_cols].astype(jnp.bfloat16), 'dp',...  79.3 us
    psum x1, blocking collectives, local(): squares_ffn = lax.psum(jnp.sum(resid_wide * resid_wide, axis=1), 'dp')  38.9 us
    psum x1, blocking collectives, local(): squares = lax.psum(jnp.sum(wide * wide, axis=1), 'dp')  38.6 us
    reduce_scatter x1, waiting for transfers between devices, local(): lax.psum_scatter(attn_partial.astype(jnp.bfloat16), 'tensor', scatter_dim...  34.6 us
    reduce_scatter x1, waiting for transfers between devices, local(): lax.psum_scatter(ffn_partial.astype(jnp.bfloat16), 'tensor', scatter_dime...  33.5 us
  transfers between devices with their start and end apart: 9, of which 9 were waited for; matrix products, arithmetic and copies ran while one was open for 2% of the time, Pallas kernels for 0%

profile of v1, /device:TPU:8, one launch (start us, length us, event | category | flops | bytes accessed | tf_op | source)
XLA Modules:
  0.0 707.5 jit_solution(14938330568051807353)
XLA Ops:
  6.5 0.0 copy-start
  6.5 0.0 all-gather.4.cloned.1.call-start
  6.5 7.2 %collective-permute-start = (bf16[128,512]{1,0:T(8,128)(2,1)}, bf16[128,512]{1,0:T(8,128)(2,1)S(1)}, u32[]{:S(2)}, u32[]{:S(2)}) collective-permute-start(bf16[128,512]{1,0:T(8,128)(2,1)} %bitcast.72), channel_id=1, source_target_pairs={{0,128},{128,0},{1,129},{129,1},{2,130},{130,2},{3,131},{131,3},{4... | collective-permute-start | bytes 393224 | tf_op jit(solution)/shard_map/ppermute | solution.py:16
  13.7 0.7 mul.231
  14.4 3.1 collective-permute-done
  17.5 0.1 fusion.25
  17.6 38.6 %psum.21 = f32[128]{0:T(128)S(1)} all-reduce(f32[128]{0:T(128)S(1)} %fusion.25), channel_id=1, replica_groups=mesh['section'=2,'dp'=16,'tensor'=8] {'dp'}, use_global_device_ids=true, to_apply=%region_1.2 | all-reduce | flops 128 | bytes 1024 | tf_op jit(solution)/shard_map/psum | solution.py:71
  56.2 0.8 fusion.27
  57.0 0.0 all-gather.4.cloned.1.call-update
  57.0 0.0 all-reduce.2.cloned.1.call-start
  57.1 1.7 dynamic-slice_bitcast_fusion.1
  58.8 27.4 %all-gather.4.cloned.1.call-done = bf16[1024,512]{1,0:T(8,128)(2,1)} async-done(((bf16[128,512]{1,0:T(8,128)(2,1)}), bf16[1024,512]{1,0:T(8,128)(2,1)}) %all-gather.4.cloned.1.call-update) | async-done | bytes 1048592 | tf_op jit(solution)/shard_map/all_gather | solution.py:76
  86.2 2.4 convolution_convert_fusion.1
  88.7 0.8 slice.54
  89.5 0.0 all-reduce.2.cloned.1.call-update
  89.5 0.0 reduce-scatter.5.cloned.1.call-start
  89.6 1.1 slice.59
  90.6 0.0 reduce-scatter.5.cloned.1.call-update
  90.7 0.0 reduce-scatter.7.cloned.1.call-start
  90.8 0.1 iota_compare_fusion
  90.9 0.2 multiply_cosine_fusion.1
  91.1 160.4 %all-reduce.2.cloned.1.call-done = bf16[1024,256]{1,0:T(8,128)(2,1)} async-done(((bf16[1024,256]{1,0:T(8,128)(2,1)}), bf16[1024,256]{1,0:T(8,128)(2,1)}) %all-reduce.2.cloned.1.call-update) | async-done | bytes 524304 | tf_op jit(solution)/shard_map/psum | solution.py:83
  251.5 1.1 fusion.33
  252.6 2.4 fusion.37
  255.0 79.3 %reduce-scatter.5.cloned.1.call-done = bf16[64,512]{1,0:T(8,128)(2,1)} async-done(((bf16[1024,512]{1,0:T(8,128)(2,1)}), bf16[64,512]{1,0:T(8,128)(2,1)}) %reduce-scatter.5.cloned.1.call-update) | async-done | bytes 65552 | tf_op jit(solution)/shard_map/reduce_scatter | solution.py:80
  334.4 0.9 reshape.222
  335.2 0.1 fusion.45
  335.4 0.6 fusion.46
  336.0 0.0 copy-done.2
  336.0 0.0 copy-start.4
  336.0 0.4 fusion.8
  336.4 0.1 copy.13
  336.4 0.1 stack.3
  336.5 0.0 copy-start.3
  336.6 23.4 %all_to_all.5 = bf16[16,64,512]{2,1,0:T(8,128)(2,1)S(1)} all-to-all(bf16[16,64,512]{2,1,0:T(8,128)(2,1)S(1)} %stack.3), channel_id=1, replica_groups=mesh['section'=2,'dp'=16,'tensor'=8] {'dp'}, dimensions={0} | all-to-all | bytes 2097152 | tf_op jit(solution)/shard_map/all_to_all | solution.py:105
  360.0 0.0 copy-done.4
  360.0 1.7 convolution_convert_fusion.2
  361.7 0.0 reduce-scatter.7.cloned.1.call-update
  361.7 0.0 all-gather.6.cloned.1.call-start
  361.7 0.0 copy-done.3
  361.8 34.6 %reduce-scatter.7.cloned.1.call-done = bf16[128,512]{1,0:T(8,128)(2,1)} async-done(((bf16[1024,512]{1,0:T(8,128)(2,1)}), bf16[128,512]{1,0:T(8,128)(2,1)}) %reduce-scatter.7.cloned.1.call-update) | async-done | bytes 131088 | tf_op jit(solution)/shard_map/reduce_scatter | solution.py:110
  396.3 1.0 fusion.29
  397.4 38.9 %psum.23 = f32[128]{0:T(128)S(1)} all-reduce(f32[128]{0:T(128)S(1)} %fusion.29), channel_id=1, replica_groups=mesh['section'=2,'dp'=16,'tensor'=8] {'dp'}, use_global_device_ids=true, to_apply=%region_7.8 | all-reduce | flops 128 | bytes 1024 | tf_op jit(solution)/shard_map/psum | solution.py:115
  436.3 1.7 fusion.31
  438.0 0.0 all-gather.6.cloned.1.call-update
  438.0 0.0 reduce-scatter.9.cloned.1.call-start
  438.0 6.0 copy.14
  444.0 18.2 %all-gather.6.cloned.1.call-done = bf16[1024,512]{1,0:T(8,128)(2,1)} async-done(((bf16[128,512]{1,0:T(8,128)(2,1)}), bf16[1024,512]{1,0:T(8,128)(2,1)}) %all-gather.6.cloned.1.call-update) | async-done | bytes 1048592 | tf_op jit(solution)/shard_map/all_gather | solution.py:119
  462.2 9.3 %convolution_convert_fusion = bf16[1024,3584]{1,0:T(8,128)(2,1)} fusion(bf16[1024,512]{1,0:T(8,128)(2,1)} %all-gather.6.cloned.1.call-done, bf16[3584,512]{1,0:T(8,128)(2,1)} %bitcast.65), kind=kOutput, calls=%fused_computation | convolution fusion | flops 3761766400 | bytes 12058624 | tf_op jit(solution)/shard_map/rd,gdf->rgf/dot_general | solution.py:122
  471.5 0.0 reduce-scatter.9.cloned.1.call-update
  471.5 0.0 all-gather.8.cloned.1.call-start
  471.6 100.8 %reduce-scatter.9.cloned.1.call-done = bf16[64,3584]{1,0:T(8,128)(2,1)} async-done(((bf16[1024,3584]{1,0:T(8,128)(2,1)}), bf16[64,3584]{1,0:T(8,128)(2,1)}) %reduce-scatter.9.cloned.1.call-update) | async-done | bytes 458768 | tf_op jit(solution)/shard_map/reduce_scatter | solution.py:121
  572.4 1.1 convert_element_type.103
  573.5 0.8 fusion.24
  574.3 0.0 all-gather.8.cloned.1.call-update
  574.3 0.0 copy-start.1
  574.3 0.0 reduce-scatter.11.cloned.1.call-start
  574.4 86.1 %all-gather.8.cloned.1.call-done = bf16[1024,1792]{1,0:T(8,128)(2,1)} async-done(((bf16[64,1792]{1,0:T(8,128)(2,1)}), bf16[1024,1792]{1,0:T(8,128)(2,1)}) %all-gather.8.cloned.1.call-update) | async-done | bytes 3670032 | tf_op jit(solution)/shard_map/all_gather | solution.py:131
  660.5 0.0 copy-done
  660.5 5.1 fusion.2
  665.6 0.0 reduce-scatter.11.cloned.1.call-update
  665.6 33.5 %reduce-scatter.11.cloned.1.call-done = bf16[128,512]{1,0:T(8,128)(2,1)} async-done(((bf16[1024,512]{1,0:T(8,128)(2,1)}), bf16[128,512]{1,0:T(8,128)(2,1)}) %reduce-scatter.11.cloned.1.call-update) | async-done | bytes 131088 | tf_op jit(solution)/shard_map/reduce_scatter | solution.py:135
  699.1 0.0 copy-done.1
  699.1 1.6 fusion.38
  (10 shorter events, 0.1 us)
Async XLA Ops:
  6.5 654.0 %copy-start = (bf16[1,1792,512]{2,1,0:T(8,128)(2,1)S(1)}, bf16[1,1792,512]{2,1,0:T(8,128)(2,1)}, u32[]{:S(2)}) copy-start(bf16[1,1792,512]{2,1,0:T(8,128)(2,1)} %param.15) | copy-start | bytes 5505028
  6.5 79.7 %all-gather.4.cloned.1.call-start = ((), (), s32[]{:S(2)}) async-start(), calls=%async_computation.5 | async-start | bytes 1179648 | tf_op jit(solution)/shard_map/all_gather | solution.py:76
  6.5 11.0 %collective-permute-start = (bf16[128,512]{1,0:T(8,128)(2,1)}, bf16[128,512]{1,0:T(8,128)(2,1)S(1)}, u32[]{:S(2)}, u32[]{:S(2)}) collective-permute-start(bf16[128,512]{1,0:T(8,128)(2,1)} %bitcast.72), channel_id=1, source_target_pairs={{0,128},{128,0},{1,129},{129,1},{2,130},{130,2},{3,131},{131,3},{4... | collective-permute-start | bytes 393224 | tf_op jit(solution)/shard_map/ppermute | solution.py:16
  57.0 194.5 %all-reduce.2.cloned.1.call-start = ((), (), s32[]{:S(2)}) async-start(), calls=%async_computation.6 | async-start | bytes 1048576 | tf_op jit(solution)/shard_map/psum | solution.py:83
  89.5 244.8 %reduce-scatter.5.cloned.1.call-start = ((), (), s32[]{:S(2)}) async-start(), calls=%async_computation.7 | async-start | bytes 1114112 | tf_op jit(solution)/shard_map/reduce_scatter | solution.py:80
  90.7 305.7 %reduce-scatter.7.cloned.1.call-start = ((), (), s32[]{:S(2)}) async-start(), calls=%async_computation.8 | async-start | bytes 1179648 | tf_op jit(solution)/shard_map/reduce_scatter | solution.py:110
  251.5 84.5 %copy-start.2 = (bf16[1024,256]{1,0:T(8,128)(2,1)S(1)}, bf16[1024,256]{1,0:T(8,128)(2,1)}, u32[]{:S(2)}) copy-start(bf16[1024,256]{1,0:T(8,128)(2,1)} %all-reduce.2.cloned.1.call-done) | copy-start | bytes 1572868
  336.0 24.0 %copy-start.4 = (bf16[1,512,512]{2,1,0:T(8,128)(2,1)S(1)}, bf16[1,512,512]{2,1,0:T(8,128)(2,1)}, u32[]{:S(2)}) copy-start(bf16[1,512,512]{2,1,0:T(8,128)(2,1)} %param.12) | copy-start | bytes 1572868
  336.5 25.2 %copy-start.3 = (bf16[1,512]{1,0:T(2,128)(2,1)S(1)}, bf16[1,512]{1,0:T(2,128)(2,1)}, u32[]{:S(2)}) copy-start(bf16[1,512]{1,0:T(2,128)(2,1)} %param.13) | copy-start | bytes 3076
  361.7 100.5 %all-gather.6.cloned.1.call-start = ((), (), s32[]{:S(2)}) async-start(), calls=%async_computation.9 | async-start | bytes 1179648 | tf_op jit(solution)/shard_map/all_gather | solution.py:119
  438.0 134.4 %reduce-scatter.9.cloned.1.call-start = ((), (), s32[]{:S(2)}) async-start(), calls=%async_computation.10 | async-start | bytes 7798784 | tf_op jit(solution)/shard_map/reduce_scatter | solution.py:121
  471.5 189.0 %all-gather.8.cloned.1.call-start = ((), (), s32[]{:S(2)}) async-start(), calls=%async_computation.11 | async-start | bytes 3899392 | tf_op jit(solution)/shard_map/all_gather | solution.py:131
  574.3 124.8 %copy-start.1 = (bf16[128,512]{1,0:T(8,128)(2,1)S(1)}, bf16[128,512]{1,0:T(8,128)(2,1)}, u32[]{:S(2)}) copy-start(bf16[128,512]{1,0:T(8,128)(2,1)} %reduce-scatter.7.cloned.1.call-done) | copy-start | bytes 393220
  574.3 124.7 %reduce-scatter.11.cloned.1.call-start = ((), (), s32[]{:S(2)}) async-start(), calls=%async_computation.12 | async-start | bytes 1179648 | tf_op jit(solution)/shard_map/reduce_scatter | solution.py:135
Sparse Core Ops, SparseCore 0:
  57.2 29.0 all-gather.3
  89.7 161.8 all-reduce.1
  254.0 80.2 reduce-scatter.4
  361.8 34.4 reduce-scatter.6
  438.1 24.0 all-gather.5
  471.7 100.7 reduce-scatter.8
  574.5 86.0 all-gather.7
  665.8 33.2 reduce-scatter.10
